TPU v7x, 32 devices: a whole 2x2x4 slice. The times are simulated.
32 devices in a mesh: dp: 4 (over z), group: 8 (over y, x, core).
Axes of the slice: x: 2, y: 2, z: 4, core: 2. Of those that a mesh axis runs over, the one named last changes fastest.
Arguments:
- tokens: bfloat16 [128, 160, 768], P(('dp', 'group')), may hold values from -6 to 6
- cotangent: bfloat16 [128, 160, 768], P(('dp', 'group')), may hold values from -6 to 6
- counts: int32 [128], P(('dp', 'group')), may hold values from 96 to 160, as said below
- first_gain: float32 [768], replicated, may hold values from 0.5 to 1.5
- first_shift: float32 [768], replicated, may hold values from -1.75 to 1.75
- joined_weight: bfloat16 [768, 2304], replicated, may hold values from -0.21875 to 0.21875
- joined_bias: float32 [2, 768], replicated, may hold values from -1.75 to 1.75
- merge_weight: bfloat16 [768, 768], replicated, may hold values from -0.75 to 0.75
- merge_bias: float32 [768], replicated, may hold values from -1.75 to 1.75
- second_gain: float32 [768], replicated, may hold values from 0.5 to 1.5
- second_shift: float32 [768], replicated, may hold values from -1.75 to 1.75
- up_weight: bfloat16 [768, 3072], replicated, may hold values from -0.21875 to 0.21875
- up_bias: float32 [3072], replicated, may hold values from -1.75 to 1.75
- down_weight: bfloat16 [3072, 768], replicated, may hold values from -0.109375 to 0.109375
- down_bias: float32 [768], replicated, may hold values from -1.75 to 1.75
Outputs:
- result: bfloat16 [128, 160, 768], P(('dp', 'group'))
- token_grad: bfloat16 [128, 160, 768], P(('dp', 'group'))
- first_gain_grad: float32 [768], replicated
- first_shift_grad: float32 [768], replicated
- joined_weight_grad: float32 [768, 2304], replicated
- joined_bias_grad: float32 [2, 768], replicated
- merge_weight_grad: float32 [768, 768], replicated
- merge_bias_grad: float32 [768], replicated
- second_gain_grad: float32 [768], replicated
- second_shift_grad: float32 [768], replicated
- up_weight_grad: float32 [768, 3072], replicated
- up_bias_grad: float32 [3072], replicated
- down_weight_grad: float32 [3072, 768], replicated
- down_bias_grad: float32 [768], replicated
Inputs may be any that keep to these rules, and one draw needn't show every extreme that they name: `counts`: item j of a device is owned by the device with index j // 1 along dp and the same index along group; the items owned by one device hold 512 visible patches together.
All inputs are finite; a program needn't handle non-finite values.
Results may differ from a plain program's by a relative error of at most 0.012.
Values may be sent and summed in bfloat16 or wider, within the bound.
No kernel may reach another device: no remote copies, remote signals or barrier semaphores. Data moves between devices by JAX's collectives and lax.ppermute only.
A program may use at most 256 MiB of HBM per device.

v0:
```python
import jax
import jax.numpy as jnp
from jax import lax
from jax.sharding import PartitionSpec as P

HEADS = 12
HEAD_DIM = 64
VIS_MEAN = 128
EPS = 1e-06
NEG = -1e30


def norm_rows(matrix, gain_row, shift_row):
    row_mean = jnp.mean(matrix, axis=-1, keepdims=True)
    centred = matrix - row_mean
    variance = jnp.mean(centred * centred, axis=-1, keepdims=True)
    return centred * lax.rsqrt(variance + EPS) * gain_row + shift_row


def exact_gelu(matrix):
    return jax.nn.gelu(matrix, approximate=False)


def rows_inner(left, right):
    return lax.dot_general(
        left, right, (((0,), (0,)), ((), ())), preferred_element_type=jnp.float32
    )


def rows_back(left, right):
    return lax.dot_general(
        left, right, (((1,), (1,)), ((), ())), preferred_element_type=jnp.float32
    )


def attend(queries, key_rows, values, allowed):
    factor = HEAD_DIM ** (-0.5)
    scores = (
        jnp.einsum("qhd,khd->hqk", queries, key_rows, preferred_element_type=jnp.float32) * factor
    )
    scores = jnp.where(allowed[None], scores, NEG)
    highest = jnp.max(scores, axis=-1, keepdims=True)
    raised = jnp.exp(scores - highest)
    row_total = jnp.sum(raised, axis=-1, keepdims=True)
    probs_low = (raised / row_total).astype(jnp.bfloat16)
    mixture = jnp.einsum("hqk,khd->qhd", probs_low, values, preferred_element_type=jnp.float32)
    return (mixture, highest[..., 0] + jnp.log(row_total[..., 0]))


def attend_back(queries, key_rows, values, allowed, logsum, grad_mixture):
    factor = HEAD_DIM ** (-0.5)
    scores = (
        jnp.einsum("qhd,khd->hqk", queries, key_rows, preferred_element_type=jnp.float32) * factor
    )
    scores = jnp.where(allowed[None], scores, NEG)
    soft = jnp.exp(scores - logsum[..., None])
    soft_low = soft.astype(jnp.bfloat16)
    grad_probs = jnp.einsum(
        "qhd,khd->hqk", grad_mixture, values, preferred_element_type=jnp.float32
    )
    grad_scores = soft * (grad_probs - jnp.sum(soft * grad_probs, axis=-1, keepdims=True))
    grad_low = grad_scores.astype(jnp.bfloat16)
    grad_queries = (
        jnp.einsum("hqk,khd->qhd", grad_low, key_rows, preferred_element_type=jnp.float32) * factor
    )
    grad_keys = (
        jnp.einsum("hqk,qhd->khd", grad_low, queries, preferred_element_type=jnp.float32) * factor
    )
    grad_values = jnp.einsum(
        "hqk,qhd->khd", soft_low, grad_mixture, preferred_element_type=jnp.float32
    )
    return (grad_queries, grad_keys, grad_values)


def layer(packed, cot_rows, visible, weights, attention, attention_back, settle_mlp):
    (
        first_gain,
        first_shift,
        joined_weight,
        joined_bias,
        merge_weight,
        merge_bias,
        second_gain,
        second_shift,
        up_weight,
        up_bias,
        down_weight,
        down_bias,
    ) = weights
    row_count, features = packed.shape
    inputs = packed.astype(jnp.float32)
    normed, first_back = jax.vjp(norm_rows, inputs, first_gain, first_shift)
    normed_low = normed.astype(jnp.bfloat16)
    bias_full = jnp.concatenate(
        [joined_bias[0], jnp.zeros((features,), jnp.float32), joined_bias[1]]
    )
    joined = jnp.dot(normed_low, joined_weight, preferred_element_type=jnp.float32) + bias_full
    joined_low = joined.astype(jnp.bfloat16).reshape(row_count, 3, HEADS, HEAD_DIM)
    queries = joined_low[:, 0]
    key_rows = joined_low[:, 1]
    values = joined_low[:, 2]
    mixture, kept_stats = attention(queries, key_rows, values)
    mixture_low = mixture.reshape(row_count, features).astype(jnp.bfloat16)
    middle = (
        inputs + jnp.dot(mixture_low, merge_weight, preferred_element_type=jnp.float32) + merge_bias
    )
    second, second_back = jax.vjp(norm_rows, middle, second_gain, second_shift)
    second_low = second.astype(jnp.bfloat16)
    hidden = jnp.dot(second_low, up_weight, preferred_element_type=jnp.float32) + up_bias
    active, gelu_back = jax.vjp(exact_gelu, hidden)
    active_low = active.astype(jnp.bfloat16)
    outer = jnp.dot(active_low, down_weight, preferred_element_type=jnp.float32) + down_bias
    result = ((middle + outer) * visible[:, None]).astype(jnp.bfloat16)
    grad_result = cot_rows.astype(jnp.float32) * visible[:, None]
    grad_out = grad_result.astype(jnp.bfloat16)
    grad_down = rows_inner(active_low, grad_out)
    grad_down_bias = jnp.sum(grad_out.astype(jnp.float32), axis=0)
    (grad_active,) = gelu_back(rows_back(grad_out, down_weight))
    grad_hidden = grad_active.astype(jnp.bfloat16)
    grad_up = rows_inner(second_low, grad_hidden)
    grad_up_bias = jnp.sum(grad_hidden.astype(jnp.float32), axis=0)
    grad_middle, grad_second_gain, grad_second_shift = second_back(
        rows_back(grad_hidden, up_weight)
    )
    grad_middle = grad_middle + grad_result
    mlp_sums = settle_mlp(
        (grad_second_gain, grad_second_shift, grad_up, grad_up_bias, grad_down, grad_down_bias)
    )
    grad_branch = grad_middle.astype(jnp.bfloat16)
    grad_merge = rows_inner(mixture_low, grad_branch)
    grad_merge_bias = jnp.sum(grad_branch.astype(jnp.float32), axis=0)
    grad_mixture = (
        rows_back(grad_branch, merge_weight)
        .astype(jnp.bfloat16)
        .reshape(row_count, HEADS, HEAD_DIM)
    )
    grad_queries, grad_keys, grad_values = attention_back(
        queries, key_rows, values, kept_stats, grad_mixture
    )
    grad_joined = jnp.stack([grad_queries, grad_keys, grad_values], axis=1)
    grad_joined = grad_joined.reshape(row_count, 3 * features).astype(jnp.bfloat16)
    grad_joined_weight = rows_inner(normed_low, grad_joined)
    joined_sums = jnp.sum(grad_joined.astype(jnp.float32), axis=0)
    grad_joined_bias = jnp.stack([joined_sums[:features], joined_sums[2 * features :]])
    grad_inputs, grad_first_gain, grad_first_shift = first_back(
        rows_back(grad_joined, joined_weight)
    )
    grad_rows = (grad_middle + grad_inputs).astype(jnp.bfloat16)
    attn_grads = (
        grad_first_gain,
        grad_first_shift,
        grad_joined_weight,
        grad_joined_bias,
        grad_merge,
        grad_merge_bias,
    )
    return (result, grad_rows, attn_grads, mlp_sums)


def shards(
    tokens,
    cotangent,
    counts,
    first_gain,
    first_shift,
    joined_weight,
    joined_bias,
    merge_weight,
    merge_bias,
    second_gain,
    second_shift,
    up_weight,
    up_bias,
    down_weight,
    down_bias,
):
    weights = (
        first_gain,
        first_shift,
        joined_weight,
        joined_bias,
        merge_weight,
        merge_bias,
        second_gain,
        second_shift,
        up_weight,
        up_bias,
        down_weight,
        down_bias,
    )
    item_count, slot_count, features = tokens.shape
    slot_range = jnp.arange(slot_count, dtype=jnp.int32)

    def settle_mlp(parts):
        return parts

    arrived_all = (
        lax.all_to_all(tokens, "dp", split_axis=0, concat_axis=0, tiled=True),
        lax.all_to_all(cotangent, "dp", split_axis=0, concat_axis=0, tiled=True),
        lax.all_to_all(counts.astype(jnp.bfloat16), "dp", split_axis=0, concat_axis=0, tiled=True),
    )
    arrived, arrived_cot, arrived_counts = arrived_all
    arrived_counts = arrived_counts.astype(jnp.int32)
    row_ends = jnp.cumsum(arrived_counts)
    starts = row_ends - arrived_counts
    total_rows = item_count * VIS_MEAN
    position = jnp.arange(total_rows, dtype=jnp.int32)
    segment = jnp.sum((position[:, None] >= row_ends[None, :]).astype(jnp.int32), axis=1)
    member = segment[:, None] == jnp.arange(item_count, dtype=jnp.int32)[None, :]
    offset = position - jnp.sum(jnp.where(member, starts[None, :], 0), axis=1)
    source = segment * slot_count + offset
    packed = arrived.reshape(-1, features)[source]
    cot_rows = arrived_cot.reshape(-1, features)[source]
    visible = jnp.ones((total_rows,), jnp.float32)
    block = 512
    count_blocks = total_rows // block
    window = min(total_rows, (block + 2 * slot_count + 127) // 128 * 128)
    block_ids = jnp.arange(count_blocks, dtype=jnp.int32)

    def window_start(index):
        return jnp.clip(index * block - slot_count, 0, total_rows - window)

    def attention(queries, key_rows, values):

        def forward_block(pieces):
            query_block, segment_block, index = pieces
            begin = window_start(index)
            near_keys = lax.dynamic_slice_in_dim(key_rows, begin, window, 0)
            near_values = lax.dynamic_slice_in_dim(values, begin, window, 0)
            near_segment = lax.dynamic_slice_in_dim(segment, begin, window, 0)
            allowed = segment_block[:, None] == near_segment[None, :]
            return attend(query_block, near_keys, near_values, allowed)

        mixture, logsum = lax.map(
            forward_block,
            (
                queries.reshape(count_blocks, block, HEADS, HEAD_DIM),
                segment.reshape(count_blocks, block),
                block_ids,
            ),
        )
        return (mixture.reshape(total_rows, HEADS, HEAD_DIM), logsum)

    def attention_back(queries, key_rows, values, logsum, grad_mixture):

        def back_block(carry, pieces):
            query_block, segment_block, logsum_block, grad_block, index = pieces
            begin = window_start(index)
            near_keys = lax.dynamic_slice_in_dim(key_rows, begin, window, 0)
            near_values = lax.dynamic_slice_in_dim(values, begin, window, 0)
            near_segment = lax.dynamic_slice_in_dim(segment, begin, window, 0)
            allowed = segment_block[:, None] == near_segment[None, :]
            grad_queries, grad_keys, grad_values = attend_back(
                query_block, near_keys, near_values, allowed, logsum_block, grad_block
            )
            key_total = lax.dynamic_update_slice_in_dim(
                carry[0], lax.dynamic_slice_in_dim(carry[0], begin, window, 0) + grad_keys, begin, 0
            )
            value_total = lax.dynamic_update_slice_in_dim(
                carry[1],
                lax.dynamic_slice_in_dim(carry[1], begin, window, 0) + grad_values,
                begin,
                0,
            )
            return ((key_total, value_total), grad_queries)

        zeroed = jnp.zeros((total_rows, HEADS, HEAD_DIM), jnp.float32)
        (grad_keys, grad_values), grad_queries = lax.scan(
            back_block,
            (zeroed, zeroed),
            (
                queries.reshape(count_blocks, block, HEADS, HEAD_DIM),
                segment.reshape(count_blocks, block),
                logsum,
                grad_mixture.reshape(count_blocks, block, HEADS, HEAD_DIM),
                block_ids,
            ),
        )
        return (grad_queries.reshape(total_rows, HEADS, HEAD_DIM), grad_keys, grad_values)

    out_rows, grad_rows, attn_grads, mlp_sums = layer(
        packed, cot_rows, visible, weights, attention, attention_back, settle_mlp
    )
    slot_index = starts[:, None] + slot_range[None, :]
    inside = slot_range[None, :] < arrived_counts[:, None]
    picked = jnp.minimum(slot_index, total_rows - 1)
    back_out = jnp.where(inside[..., None], out_rows[picked], jnp.zeros((), jnp.bfloat16))
    back_grad = jnp.where(inside[..., None], grad_rows[picked], jnp.zeros((), jnp.bfloat16))
    returned = (
        lax.all_to_all(back_out, "dp", split_axis=0, concat_axis=0, tiled=True),
        lax.all_to_all(back_grad, "dp", split_axis=0, concat_axis=0, tiled=True),
    )
    result = returned[0]
    token_grad = returned[1]
    summed = lax.psum(attn_grads + mlp_sums, ("dp", "group"))
    return (
        result,
        token_grad,
        summed[0],
        summed[1],
        summed[2],
        summed[3],
        summed[4],
        summed[5],
        summed[6],
        summed[7],
        summed[8],
        summed[9],
        summed[10],
        summed[11],
    )


def solution(mesh):
    in_specs = (
        P(("dp", "group"), None, None),
        P(("dp", "group"), None, None),
        P(("dp", "group")),
        P(),
        P(),
        P(),
        P(),
        P(),
        P(),
        P(),
        P(),
        P(),
        P(),
        P(),
        P(),
    )
    out_specs = (
        P(("dp", "group"), None, None),
        P(("dp", "group"), None, None),
        P(),
        P(),
        P(),
        P(),
        P(),
        P(),
        P(),
        P(),
        P(),
        P(),
        P(),
        P(),
    )
    return jax.shard_map(shards, mesh=mesh, in_specs=in_specs, out_specs=out_specs, check_vma=False)
```

profile of v0, /device:TPU:0, one launch (start us, length us, event | category | flops | bytes accessed | tf_op | source)
XLA Modules:
  0.0 690.3 jit_solution(2284785976258960198)
XLA Ops:
  8.1 11.8 %all_to_all.29 = bf16[4,1,1]{2,1,0:T(2,128)(2,1)S(1)} all-to-all(bf16[4,1,1]{2,1,0:T(2,128)(2,1)S(1)} %copy.58), channel_id=1, replica_groups=mesh['dp'=4,'group'=8] {'dp'}, dimensions={0} | all-to-all | bytes 16 | tf_op jit(solution)/shard_map/all_to_all | solution.py:200
  19.9 4.2 all-to-all-start.1
  27.4 19.9 %all-to-all-done.1 = bf16[4,160,768]{2,1,0:T(8,128)(2,1)} async-done(((bf16[4,160,768]{2,1,0:T(8,128)(2,1)}), bf16[4,160,768]{2,1,0:T(8,128)(2,1)}, u32[]{:S(2)}, u32[]{:S(2)}) %all-to-all-start.1) | async-done | bytes 983072 | tf_op jit(solution)/shard_map/all_to_all | solution.py:198
  47.4 4.3 all-to-all-start.3
  51.7 4.4 gather_fusion
  60.1 4.7 fusion.12
  64.8 4.3 copy.59
  69.1 3.5 fusion.13
  72.6 3.7 fusion
  77.2 5.5 fusion.29
  82.6 4.9 gather_fusion.2
  90.6 5.5 fusion.44
  96.2 19.0 %convert_reduce_fusion = (f32[3072]{0:T(1024)}, bf16[512,3072]{1,0:T(8,128)(2,1)S(1)}, f32[512,3072]{1,0:T(8,128)}) fusion(f32[512,3072]{1,0:T(8,128)S(1)} %fusion.44, f32[3072]{0:T(1024)S(1)} %copy-done.31, bf16[512,768]{1,0:T(8,128)(2,1)S(1)} %copy-done.7, bf16[3072,768]{1,0:T(8,128)(2,1)S(1)} %bitcast.103), kind=kOutput, calls=%fused_computation.15 | convolution fusion | flops 2533880832 | bytes 21258240 | tf_op jit(solution)/shard_map/dot_general | solution.py:31
  115.2 3.5 multiply_reduce_fusion.1
  126.4 9.0 %fusion.26 = bf16[512,1,12,64]{0,3,2,1:T(8,128)(2,1)} fusion(bf16[512,12,64]{0,2,1:T(8,128)(2,1)} %bitcast.89, f32[12,512]{1,0:T(8,128)} %log_add_fusion, f32[12,512,512]{1,2,0:T(8,128)} %copy-done.1, pred[512,512]{0,1:T(8,128)(4,1)} %broadcast_compare_fusion), kind=kOutput, calls=%fused_computation.66 | convolution fusion | flops 415236096 | bytes 14442496 | tf_op jit(solution)/shard_map/while/body/eval_jaxpr/hqk,qhd->khd/dot_general | solution.py:69
  135.4 9.9 %multiply_reduce_fusion = (f32[12,512]{1,0:T(8,128)S(1)}, f32[12,512,512]{1,2,0:T(8,128)}) fusion(f32[12,512]{1,0:T(8,128)S(1)} %copy-done.21, f32[12,512,512]{1,2,0:T(8,128)} %copy-done.1, pred[512,512]{0,1:T(8,128)(4,1)S(1)} %copy-done.10, bf16[512,12,64]{0,2,1:T(8,128)(2,1)S(1)} %bitcast.90, bf16[512,3,12,64]{0,3,2,1:T(8,128)(2,1)} %bitcast.78), kind=kOutput, calls=%fused_computation.5 | convolution fusion | flops 418375680 | bytes 27049984 | tf_op jit(solution)/shard_map/while/body/eval_jaxpr/qhd,khd->hqk/dot_general | solution.py:58
  145.4 7.1 %multiply_convert_fusion = bf16[12,512,512]{1,2,0:T(8,128)(2,1)S(1)} fusion(f32[12,512,512]{1,2,0:T(8,128)} %get-tuple-element.113, f32[12,512]{1,0:T(8,128)S(1)} %get-tuple-element.112, f32[12,512]{1,0:T(8,128)S(1)} %copy-done.21, f32[12,512,512]{1,2,0:T(8,128)S(1)} %bitcast.75, pred[512,512]{0,1:T(8,128)(4,1)S(1)} %copy-done.10), kind=kLoop, calls=%fused_computation.4 | loop fusion | flops 18874368 | bytes 31768576 | tf_op jit(solution)/shard_map/while/body/eval_jaxpr/convert_element_type | solution.py:62
  159.8 5.6 fusion.43
  167.0 3.8 convert_reduce_fusion.1
  170.9 5.3 fusion.39
  176.2 5.4 fusion.52
  185.0 4.9 fusion.45
  193.5 5.2 gather_fusion.3
  198.7 7.3 %add_convert_fusion.2 = bf16[512,768]{1,0:T(8,128)(2,1)} fusion(f32[512,768]{1,0:T(8,128)} %copy-done.11, bf16[512,3072]{1,0:T(8,128)(2,1)} %copy-done.17, bf16[3072,768]{1,0:T(8,128)(2,1)} %param.28, f32[768]{0:T(1024)S(1)} %copy-done.44), kind=kOutput, calls=%fused_computation.63 | convolution fusion | flops 2417098752 | bytes 10226688 | tf_op jit(solution)/shard_map/dot_general | solution.py:112
  206.0 5.2 gather_fusion.1
  213.9 40.4 %all_to_all.30 = bf16[4,160,768]{2,1,0:T(8,128)(2,1)} all-to-all(bf16[4,160,768]{2,1,0:T(8,128)(2,1)S(1)} %get-tuple-element.106), channel_id=1, replica_groups=mesh['dp'=4,'group'=8] {'dp'}, dimensions={0} | all-to-all | bytes 1966080 | tf_op jit(solution)/shard_map/all_to_all | solution.py:290
  254.3 4.2 all-to-all-start.4
  260.7 54.2 %all-reduce = (f32[768]{0:T(1024)}, f32[768]{0:T(1024)}, f32[2,768]{1,0:T(2,128)}, f32[768]{0:T(1024)}, f32[768]{0:T(1024)}, /*index=5*/f32[768]{0:T(1024)}, f32[3072]{0:T(1024)}, f32[768]{0:T(1024)}) all-reduce(f32[768]{0:T(1024)} %get-tuple-element.62, ...), channel_id=1, replica_groups=mesh['dp'=4,'group'=8] {'dp','group'}, use_global_device_ids=true, to_apply=%region_15.16 | all-reduce | flops 9216 | bytes 73728 | tf_op jit(solution)/shard_map/psum | solution.py:295
  314.9 342.7 %all-reduce.4.cloned.1.call-done = (f32[768,2304]{1,0:T(8,128)}, f32[768,768]{1,0:T(8,128)}, f32[768,3072]{1,0:T(8,128)}, f32[3072,768]{1,0:T(8,128)}) async-done(((f32[768,2304]{1,0:T(8,128)}, f32[768,768]{1,0:T(8,128)}, f32[768,3072]{1,0:T(8,128)}, f32[3072,768]{1,0:T(8,128)}), (f32[768,2304]{1,0:T(8,128)}, f32[768,768]{1,0:T(8,128)}, f32[768,3072]{1,0:T(8,128)}, ...) | async-done | bytes 28311568 | tf_op jit(solution)/shard_map/psum | solution.py:295
  662.1 6.6 copy.77
  670.0 9.3 %copy.79 = f32[768,3072]{1,0:T(8,128)} copy(f32[768,3072]{1,0:T(8,128)} %get-tuple-element.139) | data formatting | bytes 18874368
  679.4 3.7 copy.80
  (181 shorter events, 46.2 us)
Async XLA Ops:
  7.2 52.9 %copy-start = (bf16[768,2304]{1,0:T(8,128)(2,1)S(1)}, bf16[768,2304]{1,0:T(8,128)(2,1)}, u32[]{:S(2)}) copy-start(bf16[768,2304]{1,0:T(8,128)(2,1)} %param.20) | copy-start | bytes 10616836
  19.9 27.5 %all-to-all-start.1 = ((bf16[4,160,768]{2,1,0:T(8,128)(2,1)}), bf16[4,160,768]{2,1,0:T(8,128)(2,1)}, u32[]{:S(2)}, u32[]{:S(2)}) async-start(bf16[4,160,768]{2,1,0:T(8,128)(2,1)} %param.15), calls=%async_computation.1 | async-start | bytes 1966080 | tf_op jit(solution)/shard_map/all_to_all | solution.py:198
  47.4 35.3 %all-to-all-start.3 = ((bf16[4,160,768]{2,1,0:T(8,128)(2,1)}), bf16[4,160,768]{2,1,0:T(8,128)(2,1)}, u32[]{:S(2)}, u32[]{:S(2)}) async-start(bf16[4,160,768]{2,1,0:T(8,128)(2,1)} %param.16), calls=%async_computation.3 | async-start | bytes 1966080 | tf_op jit(solution)/shard_map/all_to_all | solution.py:199
  51.6 8.5 %copy-start.28 = (f32[768]{0:T(1024)S(1)}, f32[768]{0:T(1024)}, u32[]{:S(2)}) copy-start(f32[768]{0:T(1024)} %param.18) | copy-start | bytes 9220
  51.6 8.5 %copy-start.42 = (f32[768]{0:T(1024)S(1)}, f32[768]{0:T(1024)}, u32[]{:S(2)}) copy-start(f32[768]{0:T(1024)} %param.19) | copy-start | bytes 9220
  51.7 606.0 %all-reduce.4.cloned.1.call-start = ((), (), s32[]{:S(2)}) async-start(), calls=%async_computation.5 | async-start | bytes 56623104 | tf_op jit(solution)/shard_map/psum | solution.py:295
  90.2 28.6 %copy-start.11 = (f32[512,768]{1,0:T(8,128)}, f32[512,768]{1,0:T(8,128)S(1)}, u32[]{:S(2)}) copy-start(f32[512,768]{1,0:T(8,128)S(1)} %get-tuple-element.110) | copy-start | bytes 4718596
  90.2 5.9 slice-start.12
  90.6 5.6 copy-start.7
  90.6 24.6 %slice-start.10 = ((s8[4718592]{0:T(1024)(128)(4,1)}), s8[4194304]{0:T(1024)(128)(4,1)S(1)}, s32[]{:S(2)}) async-start(s8[4718592]{0:T(1024)(128)(4,1)} %bitcast.100), calls=%async_computation.16 | async-start | bytes 8388608
  96.2 19.0 %copy-start.13 = (f32[512,3072]{1,0:T(8,128)}, f32[512,3072]{1,0:T(8,128)S(1)}, u32[]{:S(2)}) copy-start(f32[512,3072]{1,0:T(8,128)S(1)} %fusion.44) | copy-start | bytes 18874372
  96.2 19.0 %slice-start.11 = ((s8[4718592]{0:T(1024)(128)(4,1)}), s8[524288]{0:T(1024)(128)(4,1)S(1)}, s32[]{:S(2)}) async-start(s8[4718592]{0:T(1024)(128)(4,1)} %bitcast.100), calls=%async_computation.17 | async-start | bytes 1048576
  126.4 9.0 %copy-start.10 = (pred[512,512]{0,1:T(8,128)(4,1)S(1)}, pred[512,512]{0,1:T(8,128)(4,1)}, u32[]{:S(2)}) copy-start(pred[512,512]{0,1:T(8,128)(4,1)} %broadcast_compare_fusion) | copy-start | bytes 786436
  126.4 9.0 %copy-start.14 = (bf16[512,768]{0,1:T(8,128)(2,1)S(1)}, bf16[512,768]{0,1:T(8,128)(2,1)}, u32[]{:S(2)}) copy-start(bf16[512,768]{0,1:T(8,128)(2,1)} %copy.61) | copy-start | bytes 2359300
  126.4 9.0 %copy-start.21 = (f32[12,512]{1,0:T(8,128)S(1)}, f32[12,512]{1,0:T(8,128)}, u32[]{:S(2)}) copy-start(f32[12,512]{1,0:T(8,128)} %log_add_fusion) | copy-start | bytes 73732
  126.4 18.9 %slice-start = ((s8[12582912]{0:T(1024)(128)(4,1)}), s8[4194304]{0:T(1024)(128)(4,1)S(1)}, s32[]{:S(2)}) async-start(s8[12582912]{0:T(1024)(128)(4,1)} %bitcast.74), calls=%async_computation.6 | async-start | bytes 8388608
  126.4 18.9 %slice-start.1 = ((s8[12582912]{0:T(1024)(128)(4,1)}), s8[4194304]{0:T(1024)(128)(4,1)S(1)}, s32[]{:S(2)}) async-start(s8[12582912]{0:T(1024)(128)(4,1)} %bitcast.74), calls=%async_computation.7 | async-start | bytes 8388608
  135.4 9.9 %slice-start.2 = ((s8[12582912]{0:T(1024)(128)(4,1)}), s8[4194304]{0:T(1024)(128)(4,1)S(1)}, s32[]{:S(2)}) async-start(s8[12582912]{0:T(1024)(128)(4,1)} %bitcast.74), calls=%async_computation.8 | async-start | bytes 8388608
  145.4 7.2 %copy-start.2 = (bf16[512,2304]{0,1:T(8,128)(2,1)S(1)}, bf16[512,2304]{0,1:T(8,128)(2,1)}, u32[]{:S(2)}) copy-start(bf16[512,2304]{0,1:T(8,128)(2,1)} %copy.59) | copy-start | bytes 7077892
  157.5 7.9 %slice-start.6 = ((s8[6291456]{0:T(1024)(128)(4,1)}), s8[4194304]{0:T(1024)(128)(4,1)S(1)}, s32[]{:S(2)}) async-start(s8[6291456]{0:T(1024)(128)(4,1)} %bitcast.83), calls=%async_computation.12 | async-start | bytes 8388608
  157.5 7.9 %slice-start.8 = ((s8[6291456]{0:T(1024)(128)(4,1)}), s8[4194304]{0:T(1024)(128)(4,1)S(1)}, s32[]{:S(2)}) async-start(s8[6291456]{0:T(1024)(128)(4,1)} %bitcast.85), calls=%async_computation.14 | async-start | bytes 8388608
  159.7 5.6 slice-start.7
  159.8 5.6 slice-start.9
  159.8 5.6 copy-start.32
  167.0 9.2 %copy-start.17 = (bf16[512,3072]{1,0:T(8,128)(2,1)}, bf16[512,3072]{1,0:T(8,128)(2,1)S(1)}, u32[]{:S(2)}) copy-start(bf16[512,3072]{1,0:T(8,128)(2,1)S(1)} %multiply_convert_fusion.1) | copy-start | bytes 9437188
  185.0 6.2 copy-start.6
  185.0 6.2 copy-start.9
  254.3 60.6 %all-to-all-start.4 = ((bf16[4,160,768]{2,1,0:T(8,128)(2,1)}), bf16[4,160,768]{2,1,0:T(8,128)(2,1)}, u32[]{:S(2)}, u32[]{:S(2)}) async-start(bf16[4,160,768]{2,1,0:T(8,128)(2,1)} %get-tuple-element.105), calls=%async_computation.4 | async-start | bytes 1966080 | tf_op jit(solution)/shard_map/all_to_all | solution.py:291
  662.1 6.6 copy-start.18
  668.6 10.7 %slice-start.3 = ((s8[9437184]{0:T(1024)(128)(4,1)}), s8[4194304]{0:T(1024)(128)(4,1)S(1)}, s32[]{:S(2)}) async-start(s8[9437184]{0:T(1024)(128)(4,1)} %bitcast.81), calls=%async_computation.9 | async-start | bytes 8388608
  670.0 9.3 %slice-start.4 = ((s8[9437184]{0:T(1024)(128)(4,1)}), s8[4194304]{0:T(1024)(128)(4,1)S(1)}, s32[]{:S(2)}) async-start(s8[9437184]{0:T(1024)(128)(4,1)} %bitcast.81), calls=%async_computation.10 | async-start | bytes 8388608
  670.0 9.3 %slice-start.5 = ((s8[9437184]{0:T(1024)(128)(4,1)}), s8[1048576]{0:T(1024)(128)(4,1)S(1)}, s32[]{:S(2)}) async-start(s8[9437184]{0:T(1024)(128)(4,1)} %bitcast.81), calls=%async_computation.11 | async-start | bytes 2097152
  (33 other events, 116.6 us)
Sparse Core Ops, SparseCore 0:
  181.7 475.8 all-reduce.3
where the time goes:
time: 700 us; the launch traced here: 690 us
  waiting for transfers between devices  363 us (52%)
  blocking collectives  106 us (15%)
  matrix products  101 us (14%)
  local copies, waits for them, and re-layouts  58.6 us (8%)
  other arithmetic  34.2 us (5%)
  between operations  15.1 us (2%)
  starting transfers between devices  12.8 us (2%)
    psum x1, waiting for transfers between devices, shards(): summed = lax.psum(attn_grads + mlp_sums, ('dp', 'group'))  343 us
    psum x1, blocking collectives, shards(): summed = lax.psum(attn_grads + mlp_sums, ('dp', 'group'))  54.2 us
    all_to_all x1, blocking collectives, shards(): lax.all_to_all(back_out, 'dp', split_axis=0, concat_axis=0, tiled=True)  40.4 us
    unnamed x128, local copies, waits for them, and re-layouts  29.3 us
    dot_general x4, matrix products, rows_back(): lax.dot_general(left, right, (((1,), (1,)), ((), ())), preferred_element_...  29.1 us
    all_to_all x1, waiting for transfers between devices, shards(): lax.all_to_all(tokens, 'dp', split_axis=0, concat_axis=0, tiled=True)  19.9 us
    dot_general x4, matrix products, rows_inner(): lax.dot_general(left, right, (((0,), (0,)), ((), ())), preferred_element_...  18.5 us
  transfers between devices with their start and end apart: 4, of which 2 were waited for; matrix products, arithmetic and copies ran while one was open for 10% of the time, Pallas kernels for 0%

commit v1 on v0

--- a/solution.py
+++ b/solution.py
@@ -8,6 +8,11 @@
 VIS_MEAN = 128
 EPS = 1e-06
 NEG = -1e30
+
+
+def one_after_other(x, first, second_2):
+    half = lax.psum(x, first)
+    return lax.psum(half, second_2)
 
 
 def norm_rows(matrix, gain_row, shift_row):
@@ -292,7 +297,7 @@
     )
     result = returned[0]
     token_grad = returned[1]
-    summed = lax.psum(attn_grads + mlp_sums, ("dp", "group"))
+    summed = one_after_other(attn_grads + mlp_sums, "group", "dp")
     return (
         result,
         token_grad,

time: 700 us -> 1550 us (2.21)
  waiting for transfers between devices: 363 us -> 1190 us
  blocking collectives: 106 us -> 136 us
    psum x1 -> x2, waiting for transfers between devices: 343 us -> 1170 us  [the longest x1 821 us: one_after_other(): return lax.psum(half, second_2)]
    all_to_all x1, blocking collectives: 40.4 us -> 59.2 us  [shards(): lax.all_to_all(back_out, 'dp', split_axis=0, concat_axis=0, tiled=True)]
    psum x1 -> x2, blocking collectives: 54.2 us -> 65.5 us  [the longest x1 40.1 us: one_after_other(): return lax.psum(half, second_2)]
  transfers between devices with their start and end apart: 4 -> 5, of which waited for: 2 -> 3; matrix products, arithmetic and copies ran while one was open for 10% -> 4% of each run, Pallas kernels for 0% -> 0%
where the time goes in v1:
time: 1550 us; the launch traced here: 1540 us
  waiting for transfers between devices  1190 us (77%)
  blocking collectives  136 us (9%)
  matrix products  100 us (6%)
  local copies, waits for them, and re-layouts  58.6 us (4%)
  other arithmetic  34 us (2%)
    psum x1, waiting for transfers between devices, one_after_other(): return lax.psum(half, second_2)  821 us
    psum x1, waiting for transfers between devices, one_after_other(): half = lax.psum(x, first)  345 us
    all_to_all x1, blocking collectives, shards(): lax.all_to_all(back_out, 'dp', split_axis=0, concat_axis=0, tiled=True)  59.2 us
    psum x1, blocking collectives, one_after_other(): return lax.psum(half, second_2)  40.1 us
  transfers between devices with their start and end apart: 5, of which 3 were waited for; matrix products, arithmetic and copies ran while one was open for 4% of the time, Pallas kernels for 0%

profile of v1, /device:TPU:0, one launch (start us, length us, event | category | flops | bytes accessed | tf_op | source)
XLA Modules:
  0.0 1543.5 jit_solution(14187627019302548678)
XLA Ops:
  8.1 11.8 all_to_all.29
  19.9 4.2 all-to-all-start.1
  27.4 19.9 %all-to-all-done.1 = bf16[4,160,768]{2,1,0:T(8,128)(2,1)} async-done(((bf16[4,160,768]{2,1,0:T(8,128)(2,1)}), bf16[4,160,768]{2,1,0:T(8,128)(2,1)}, u32[]{:S(2)}, u32[]{:S(2)}) %all-to-all-start.1) | async-done | bytes 983072 | tf_op jit(solution)/shard_map/all_to_all | solution.py:203
  47.4 4.3 all-to-all-start.3
  51.7 4.4 gather_fusion
  60.1 4.7 fusion.12
  64.8 4.3 copy.59
  72.6 3.7 fusion
  77.1 5.5 fusion.29
  82.6 4.9 gather_fusion.2
  90.6 5.5 fusion.44
  96.2 19.0 %convert_reduce_fusion = (f32[3072]{0:T(1024)}, bf16[512,3072]{1,0:T(8,128)(2,1)S(1)}, f32[512,3072]{1,0:T(8,128)}) fusion(f32[512,3072]{1,0:T(8,128)S(1)} %fusion.44, f32[3072]{0:T(1024)S(1)} %copy-done.31, bf16[512,768]{1,0:T(8,128)(2,1)S(1)} %copy-done.7, bf16[3072,768]{1,0:T(8,128)(2,1)S(1)} %bitcast.103), kind=kOutput, calls=%fused_computation.15 | convolution fusion | flops 2533880832 | bytes 21258240 | tf_op jit(solution)/shard_map/dot_general | solution.py:36
  126.5 9.0 fusion.26
  135.5 9.9 multiply_reduce_fusion
  145.4 7.1 multiply_convert_fusion
  159.8 5.6 fusion.43
  167.0 3.8 convert_reduce_fusion.1
  170.8 5.3 fusion.39
  176.1 5.4 fusion.52
  181.6 344.8 %all-reduce.7.cloned.1.call-done = (f32[768,2304]{1,0:T(8,128)}, f32[768,768]{1,0:T(8,128)}, f32[768,3072]{1,0:T(8,128)}, f32[3072,768]{1,0:T(8,128)}) async-done(((f32[768,2304]{1,0:T(8,128)}, f32[768,768]{1,0:T(8,128)}, f32[768,3072]{1,0:T(8,128)}, f32[3072,768]{1,0:T(8,128)}), (f32[768,2304]{1,0:T(8,128)}, f32[768,768]{1,0:T(8,128)}, f32[768,3072]{1,0:T(8,128)}, ...) | async-done | bytes 28311568 | tf_op jit(solution)/shard_map/psum | solution.py:14
  529.8 4.9 fusion.45
  538.2 5.2 gather_fusion.3
  543.4 7.2 add_convert_fusion.2
  550.6 5.2 gather_fusion.1
  558.4 59.2 %all_to_all.30 = bf16[4,160,768]{2,1,0:T(8,128)(2,1)} all-to-all(bf16[4,160,768]{2,1,0:T(8,128)(2,1)S(1)} %get-tuple-element.118), channel_id=1, replica_groups=mesh['dp'=4,'group'=8] {'dp'}, dimensions={0} | all-to-all | bytes 1966080 | tf_op jit(solution)/shard_map/all_to_all | solution.py:295
  617.6 4.2 all-to-all-start.4
  624.0 25.5 %all-reduce = (f32[768]{0:T(1024)}, f32[768]{0:T(1024)}, f32[2,768]{1,0:T(2,128)S(1)}, f32[768]{0:T(1024)}, f32[768]{0:T(1024)}, /*index=5*/f32[768]{0:T(1024)}, f32[3072]{0:T(1024)}, f32[768]{0:T(1024)}) all-reduce(f32[768]{0:T(1024)} %get-tuple-element.62, ...), channel_id=1, replica_groups=mesh['dp'=4,'group'=8] {'group'}, use_global_device_ids=true, to_apply=%region_15.16 | all-reduce | flops 9216 | bytes 73728 | tf_op jit(solution)/shard_map/psum | solution.py:14
  649.4 40.1 %all-reduce.2 = (f32[768]{0:T(1024)}, f32[768]{0:T(1024)}, f32[2,768]{1,0:T(2,128)}, f32[768]{0:T(1024)}, f32[768]{0:T(1024)}, /*index=5*/f32[768]{0:T(1024)}, f32[3072]{0:T(1024)}, f32[768]{0:T(1024)}) all-reduce(f32[768]{0:T(1024)} %get-tuple-element.80, f32[768]{0:T(1024)} %get-tuple-element.81, ...), channel_id=1, replica_groups=mesh['dp'=4,'group'=8] {'dp'}, use_global_device_ids=true, to_apply=%region_16.17 | all-reduce | flops 9216 | bytes 73728 | tf_op jit(solution)/shard_map/psum | solution.py:15
  689.5 821.3 %all-reduce.9.cloned.1.call-done = (f32[768,2304]{1,0:T(8,128)}, f32[768,768]{1,0:T(8,128)}, f32[768,3072]{1,0:T(8,128)}, f32[3072,768]{1,0:T(8,128)}) async-done(((f32[768,2304]{1,0:T(8,128)}, f32[768,768]{1,0:T(8,128)}, f32[768,3072]{1,0:T(8,128)}, f32[3072,768]{1,0:T(8,128)}), (f32[768,2304]{1,0:T(8,128)}, f32[768,768]{1,0:T(8,128)}, f32[768,3072]{1,0:T(8,128)}, ...) | async-done | bytes 28311568 | tf_op jit(solution)/shard_map/psum | solution.py:15
  1515.2 6.6 copy.81
  1523.2 9.3 copy.83
  1532.6 3.7 copy.84
  (185 shorter events, 53.2 us)
Async XLA Ops:
  7.2 52.9 %copy-start = (bf16[768,2304]{1,0:T(8,128)(2,1)S(1)}, bf16[768,2304]{1,0:T(8,128)(2,1)}, u32[]{:S(2)}) copy-start(bf16[768,2304]{1,0:T(8,128)(2,1)} %param.20) | copy-start | bytes 10616836
  19.9 27.5 %all-to-all-start.1 = ((bf16[4,160,768]{2,1,0:T(8,128)(2,1)}), bf16[4,160,768]{2,1,0:T(8,128)(2,1)}, u32[]{:S(2)}, u32[]{:S(2)}) async-start(bf16[4,160,768]{2,1,0:T(8,128)(2,1)} %param.15), calls=%async_computation.1 | async-start | bytes 1966080 | tf_op jit(solution)/shard_map/all_to_all | solution.py:203
  47.4 35.3 %all-to-all-start.3 = ((bf16[4,160,768]{2,1,0:T(8,128)(2,1)}), bf16[4,160,768]{2,1,0:T(8,128)(2,1)}, u32[]{:S(2)}, u32[]{:S(2)}) async-start(bf16[4,160,768]{2,1,0:T(8,128)(2,1)} %param.16), calls=%async_computation.3 | async-start | bytes 1966080 | tf_op jit(solution)/shard_map/all_to_all | solution.py:204
  51.6 8.5 copy-start.28
  51.6 8.5 copy-start.42
  51.7 474.7 %all-reduce.7.cloned.1.call-start = ((), (), s32[]{:S(2)}) async-start(), calls=%async_computation.5 | async-start | bytes 56623104 | tf_op jit(solution)/shard_map/psum | solution.py:14
  90.2 28.6 %copy-start.11 = (f32[512,768]{1,0:T(8,128)}, f32[512,768]{1,0:T(8,128)S(1)}, u32[]{:S(2)}) copy-start(f32[512,768]{1,0:T(8,128)S(1)} %get-tuple-element.122) | copy-start | bytes 4718596
  90.2 5.9 slice-start.12
  90.6 24.6 %slice-start.10 = ((s8[4718592]{0:T(1024)(128)(4,1)}), s8[4194304]{0:T(1024)(128)(4,1)S(1)}, s32[]{:S(2)}) async-start(s8[4718592]{0:T(1024)(128)(4,1)} %bitcast.100), calls=%async_computation.17 | async-start | bytes 8388608
  96.2 19.0 %copy-start.13 = (f32[512,3072]{1,0:T(8,128)}, f32[512,3072]{1,0:T(8,128)S(1)}, u32[]{:S(2)}) copy-start(f32[512,3072]{1,0:T(8,128)S(1)} %fusion.44) | copy-start | bytes 18874372
  96.2 19.0 %slice-start.11 = ((s8[4718592]{0:T(1024)(128)(4,1)}), s8[524288]{0:T(1024)(128)(4,1)S(1)}, s32[]{:S(2)}) async-start(s8[4718592]{0:T(1024)(128)(4,1)} %bitcast.100), calls=%async_computation.18 | async-start | bytes 1048576
  126.5 9.0 copy-start.10
  126.5 9.0 copy-start.14
  126.5 9.0 copy-start.21
  126.5 18.9 %slice-start = ((s8[12582912]{0:T(1024)(128)(4,1)}), s8[4194304]{0:T(1024)(128)(4,1)S(1)}, s32[]{:S(2)}) async-start(s8[12582912]{0:T(1024)(128)(4,1)} %bitcast.74), calls=%async_computation.7 | async-start | bytes 8388608
  126.5 18.9 %slice-start.1 = ((s8[12582912]{0:T(1024)(128)(4,1)}), s8[4194304]{0:T(1024)(128)(4,1)S(1)}, s32[]{:S(2)}) async-start(s8[12582912]{0:T(1024)(128)(4,1)} %bitcast.74), calls=%async_computation.8 | async-start | bytes 8388608
  135.5 9.9 slice-start.2
  145.4 7.2 copy-start.2
  157.5 7.8 slice-start.6
  157.5 7.8 slice-start.8
  159.7 5.6 slice-start.7
  159.7 5.6 slice-start.9
  159.7 5.6 copy-start.32
  166.9 9.2 copy-start.17
  181.6 1329.2 %all-reduce.9.cloned.1.call-start = ((), (), s32[]{:S(2)}) async-start(), calls=%async_computation.6 | async-start | bytes 56623104 | tf_op jit(solution)/shard_map/psum | solution.py:15
  529.8 6.2 copy-start.6
  529.8 6.2 copy-start.9
  617.6 71.9 %all-to-all-start.4 = ((bf16[4,160,768]{2,1,0:T(8,128)(2,1)}), bf16[4,160,768]{2,1,0:T(8,128)(2,1)}, u32[]{:S(2)}, u32[]{:S(2)}) async-start(bf16[4,160,768]{2,1,0:T(8,128)(2,1)} %get-tuple-element.117), calls=%async_computation.4 | async-start | bytes 1966080 | tf_op jit(solution)/shard_map/all_to_all | solution.py:296
  1515.2 6.6 copy-start.18
  1521.8 10.7 slice-start.3
  1523.2 9.3 slice-start.4
  1523.2 9.3 slice-start.5
  (34 other events, 122.2 us)
Sparse Core Ops, SparseCore 0:
  181.7 344.6 all-reduce.6
  529.3 981.4 all-reduce.8
